TPU v7x, 32 devices: a whole 2x2x4 slice. The times are simulated.
32 devices in a mesh: grp: 2 (over y), tm: 4 (over z), height: 2 (over core), head: 2 (over x).
Axes of the slice: x: 2, y: 2, z: 4, core: 2. Of those that a mesh axis runs over, the one named last changes fastest.
Arguments:
- query_video: bfloat16 [32, 16, 16, 3072], P('grp', 'height', 'tm', 'head'), parts along dimension 0, may hold values from -20 to 20
- key_video: bfloat16 [32, 16, 16, 3072], P('grp', 'height', 'tm', 'head'), parts along dimension 0, may hold values from -20 to 20
- value_video: bfloat16 [32, 16, 16, 3072], P('grp', 'height', 'tm', 'head'), parts along dimension 0, may hold values from -6 to 6
- query_text: bfloat16 [512, 3072], P('grp', 'head'), parts along dimension 0, may hold values from -20 to 20
- key_text: bfloat16 [512, 3072], P('grp', 'head'), parts along dimension 0, may hold values from -6 to 6
- value_text: bfloat16 [512, 3072], P('grp', 'head'), parts along dimension 0, may hold values from -6 to 6
- text_valid: int32 [512], P('grp'), parts along dimension 0, may hold values from 0 to 1, as said below
Outputs:
- out_video: bfloat16 [32, 16, 16, 3072], P('grp', 'height', 'tm', 'head'), parts along dimension 0
- out_text: bfloat16 [512, 3072], P('grp', 'head'), parts along dimension 0
There are 2 independent parts, one for each index of `grp`. A program takes and returns all parts, laid end to end along the dimension named above; each array names one. Nothing has to cross between parts.
Inputs may be any that keep to these rules, and one draw needn't show every extreme that they name: `text_valid`: 1 on a leading run of at least 64 positions and 0 on the rest; at least one position is 0.
All inputs are finite; a program needn't handle non-finite values.
Results may differ from a plain program's by a relative error of at most 0.0037.
Values may be sent and summed in bfloat16 or wider, within the bound.
No kernel may reach another device: no remote copies, remote signals or barrier semaphores. Data moves between devices by JAX's collectives and lax.ppermute only.
A program may use at most 192 MiB of HBM per device.

v0:
```python
import math
import jax
import jax.numpy as jnp
from jax import lax
from jax.sharding import PartitionSpec as P

HD = 128
TILE = 4


def with_halo(array, sides, width):
    for axis, dim in sides:
        devices, length = (lax.axis_size(axis), array.shape[dim])
        up = [(i, (i + 1) % devices) for i in range(devices - 1)]
        down = [(j, i) for i, j in up]
        last = lax.slice_in_dim(array, length - width, length, axis=dim)
        initial = lax.slice_in_dim(array, 0, width, axis=dim)
        before = lax.ppermute(last, axis, up)
        after = lax.ppermute(initial, axis, down)
        array = jnp.concatenate([before, array, after], axis=dim)
    return array


def into_tiles(field):
    time_tiles = field.shape[0] // TILE
    row_tiles = field.shape[1] // TILE
    col_tiles = field.shape[2] // TILE
    shaped = field.reshape(time_tiles, TILE, row_tiles, TILE, col_tiles, TILE, field.shape[3])
    shaped = shaped.transpose(0, 2, 4, 1, 3, 5, 6)
    return shaped.reshape(time_tiles, row_tiles, col_tiles, TILE**3, field.shape[3])


def from_tiles(tiles, time_tiles, row_tiles, col_tiles):
    shaped = tiles.reshape(time_tiles, row_tiles, col_tiles, TILE, TILE, TILE, tiles.shape[2])
    shaped = shaped.transpose(0, 3, 1, 4, 2, 5, 6)
    return shaped.reshape(time_tiles * TILE, row_tiles * TILE, col_tiles * TILE, tiles.shape[2])


def shards(query_video, key_video, value_video, query_text, key_text, value_text, text_valid):
    frames = query_video.shape[0]
    features = query_video.shape[3]
    head_count = features // HD
    time_tiles = frames // TILE
    row_tiles = query_video.shape[1] // TILE
    col_tiles = query_video.shape[2] // TILE
    tile_count = time_tiles * row_tiles * col_tiles
    volume = TILE**3
    text_count = query_text.shape[0]
    scale_factor = 1.0 / math.sqrt(HD)
    stacked = jnp.concatenate([key_video, value_video], axis=3)
    padded = with_halo(stacked, (("tm", 2), ("height", 1)), TILE)
    padded = jnp.pad(padded, ((TILE, TILE), (0, 0), (0, 0), (0, 0)))
    grid_shape = (time_tiles + 2, row_tiles + 2, col_tiles + 2, volume, head_count, HD)
    key_grid = into_tiles(padded[:, :, :, :features]).reshape(grid_shape)
    value_grid = into_tiles(padded[:, :, :, features:]).reshape(grid_shape)
    query_tiles = into_tiles(query_video).reshape(tile_count, volume, head_count, HD)
    slot_list = jnp.arange(27, dtype=jnp.int32)
    slot_ids = slot_list[None, :]
    numbering = jnp.arange(tile_count, dtype=jnp.int32)
    tile_time = numbering // (row_tiles * col_tiles)
    tile_row = numbering // col_tiles % row_tiles
    tile_col = numbering % col_tiles
    target_time = tile_time[:, None] + slot_ids // 9 - 1
    target_row = tile_row[:, None] + slot_ids // 3 % 3 - 1
    target_col = tile_col[:, None] + slot_ids % 3 - 1
    global_row = lax.axis_index("height") * row_tiles + target_row
    global_col = lax.axis_index("tm") * col_tiles + target_col
    inside = (target_time >= 0) & (target_time < time_tiles)
    inside = inside & (global_row >= 0) & (global_row < row_tiles * lax.axis_size("height"))
    inside = inside & (global_col >= 0) & (global_col < col_tiles * lax.axis_size("tm"))

    def window_block(grid, slot):
        zero = jnp.zeros((), jnp.int32)
        starts = (slot // 9, slot // 3 % 3, slot % 3, zero, zero, zero)
        block = lax.dynamic_slice(
            grid, starts, (time_tiles, row_tiles, col_tiles, volume, head_count, HD)
        )
        return block.reshape(tile_count, volume, head_count, HD)

    text_keys = key_text.reshape(text_count, head_count, HD)
    text_values = value_text.reshape(text_count, head_count, HD)
    text_queries = query_text.reshape(text_count, head_count, HD)
    text_open = text_valid > 0
    cross_scores = (
        jnp.einsum("qahd,khd->qhak", query_tiles, text_keys, preferred_element_type=jnp.float32)
        * scale_factor
    )
    cross_scores = jnp.where(text_open[None, None, None, :], cross_scores, -jnp.inf)

    def slot_scores(slot, allowed):
        picked = window_block(key_grid, slot)
        scores = (
            jnp.einsum("qahd,qbhd->qhab", query_tiles, picked, preferred_element_type=jnp.float32)
            * scale_factor
        )
        return jnp.where(allowed[:, None, None, None], scores, -jnp.inf)

    def peak_slot(peak, operands):
        scores = slot_scores(operands[0], operands[1])
        return (jnp.maximum(peak, jnp.max(scores, axis=3)), None)

    row_peak, unused = lax.scan(peak_slot, jnp.max(cross_scores, axis=3), (slot_list, inside.T))
    cross_probs = jnp.exp(cross_scores - row_peak[..., None])
    cross_weights = cross_probs.astype(jnp.bfloat16)
    text_part = jnp.einsum(
        "qhak,khd->qahd", cross_weights, text_values, preferred_element_type=jnp.float32
    )

    def add_slot(carry, operands):
        running, total = carry
        slot, allowed = operands
        probs = jnp.exp(slot_scores(slot, allowed) - row_peak[..., None])
        picked = window_block(value_grid, slot)
        running = running + jnp.einsum(
            "qhab,qbhd->qahd",
            probs.astype(jnp.bfloat16),
            picked,
            preferred_element_type=jnp.float32,
        )
        total = total + jnp.sum(probs, axis=3)
        return ((running, total), None)

    (summed, video_total), unused = lax.scan(
        add_slot, (text_part, jnp.sum(cross_probs, axis=3)), (slot_list, inside.T)
    )
    video_out = (summed / video_total.transpose(0, 2, 1)[..., None]).astype(jnp.bfloat16)
    out_video = from_tiles(
        video_out.reshape(tile_count, volume, features), time_tiles, row_tiles, col_tiles
    )
    flat_keys = key_video.reshape(-1, head_count, HD)
    flat_values = value_video.reshape(-1, head_count, HD)
    far_scores = (
        jnp.einsum("khd,nhd->hkn", text_queries, flat_keys, preferred_element_type=jnp.float32)
        * scale_factor
    )
    near_scores = (
        jnp.einsum("khd,jhd->hkj", text_queries, text_keys, preferred_element_type=jnp.float32)
        * scale_factor
    )
    near_scores = jnp.where(text_open[None, None, :], near_scores, -jnp.inf)
    far_peak = lax.pmax(jnp.max(far_scores, axis=2), ("tm", "height"))
    text_peak = jnp.maximum(far_peak, jnp.max(near_scores, axis=2))
    far_probs = jnp.exp(far_scores - text_peak[:, :, None])
    near_probs = jnp.exp(near_scores - text_peak[:, :, None])
    far_total = jnp.sum(far_probs, axis=2).T
    near_total = jnp.sum(near_probs, axis=2).T
    far_summed = jnp.einsum(
        "hkn,nhd->khd",
        far_probs.astype(jnp.bfloat16),
        flat_values,
        preferred_element_type=jnp.float32,
    )
    near_summed = jnp.einsum(
        "hkj,jhd->khd",
        near_probs.astype(jnp.bfloat16),
        text_values,
        preferred_element_type=jnp.float32,
    )
    whole_summed, whole_total = lax.psum((far_summed, far_total), ("tm", "height"))
    finished = (whole_summed + near_summed) / (whole_total + near_total)[:, :, None]
    out_text = finished.astype(jnp.bfloat16).reshape(text_count, features)
    return (out_video, out_text)


def solution(mesh):
    placed = (
        P("grp", "height", "tm", "head"),
        P("grp", "height", "tm", "head"),
        P("grp", "height", "tm", "head"),
        P("grp", "head"),
        P("grp", "head"),
        P("grp", "head"),
        P("grp"),
    )
    return jax.shard_map(
        shards,
        mesh=mesh,
        in_specs=placed,
        out_specs=(P("grp", "height", "tm", "head"), P("grp", "head")),
        check_vma=False,
    )
```

profile of v0, /device:TPU:0, one launch (start us, length us, event | category | flops | bytes accessed | tf_op | source)
XLA Modules:
  0.0 906.2 jit_solution(6479953430431862503)
XLA Ops:
  10.2 5.1 collective-permute-start
  16.7 65.8 %collective-permute-done = bf16[16,8,4,3072]{3,2,1,0:T(4,128)(2,1)S(1)} collective-permute-done((bf16[16,8,4,3072]{3,2,1,0:T(4,128)(2,1)S(1)}, bf16[16,8,4,3072]{3,2,1,0:T(4,128)(2,1)S(1)}, u32[]{:S(2)}, u32[]{:S(2)}) %collective-permute-start) | collective-permute-done | bytes 3145760 | tf_op jit(solution)/shard_map/ppermute | solution.py:18
  82.5 4.3 collective-permute-done.1
  88.5 7.0 pad_maximum_fusion
  95.6 5.1 fusion.69
  100.7 3.9 collective-permute-start.2
  105.8 4.2 reshape.186
  110.0 4.2 reshape.187
  118.8 5.9 multiply_reduce_fusion
  124.7 31.5 %pmax.7 = f32[12,256]{1,0:T(8,128)S(1)} all-reduce(f32[12,256]{1,0:T(8,128)S(1)} %get-tuple-element.360), channel_id=1, replica_groups=mesh['grp'=2,'tm'=4,'height'=2,'head'=2] {'tm','height'}, use_global_device_ids=true, to_apply=%region_9.10 | all-reduce | flops 3072 | bytes 24576 | tf_op jit(solution)/shard_map/pmax | solution.py:141
  156.2 4.0 fusion.27
  160.2 5.7 fusion.44
  165.9 3.2 copy.131
  169.1 4.2 reshape_reshape.12
  186.1 26.5 %psum.15 = f32[256,12]{0,1:T(8,128)S(1)} all-reduce(f32[256,12]{0,1:T(8,128)S(1)} %bitcast.156), channel_id=1, replica_groups=mesh['grp'=2,'tm'=4,'height'=2,'head'=2] {'tm','height'}, use_global_device_ids=true, to_apply=%region_13.14 | all-reduce | flops 3072 | bytes 24576 | tf_op jit(solution)/shard_map/psum | solution.py:159
  215.3 10.6 %all-reduce.3.cloned.1.call-done = f32[256,12,128]{2,0,1:T(8,128)} async-done(((f32[256,12,128]{2,0,1:T(8,128)}), f32[256,12,128]{2,0,1:T(8,128)}) %all-reduce.3.cloned.1.call-update) | async-done | bytes 1572880 | tf_op jit(solution)/shard_map/psum | solution.py:159
  226.0 4.8 fusion.36
  235.3 46.5 %select_maximum_fusion = bf16[24,16,12,3072]{3,2,1,0:T(8,128)(2,1)} fusion(bf16[16,4,12,3072]{3,2,1,0:T(8,128)(2,1)} %collective-permute-done.3, bf16[16,4,12,3072]{3,2,1,0:T(8,128)(2,1)} %collective-permute-done.2, bf16[16,8,4,3072]{3,2,1,0:T(4,128)(2,1)} %copy-done.4, bf16[16,8,4,3072]{3,2,1,0:T(4,128)(2,1)S(1)} %constant_dynamic-update-slice_fusion, ...), kind=kLoop, calls=%fused_computation.19 | loop fusion | flops 254803968 | bytes 47185920 | tf_op jit(solution)/shard_map/concatenate | solution.py:20
  281.9 26.4 %fusion.68 = (bf16[24,16,12,1536]{3,2,1,0:T(8,128)(2,1)}, bf16[24,16,12,1536]{3,2,1,0:T(8,128)(2,1)}) fusion(bf16[24,16,12,3072]{3,2,1,0:T(8,128)(2,1)} %select_maximum_fusion), kind=kLoop, calls=%fused_computation.106 | loop fusion | bytes 56623104 | tf_op jit(solution)/shard_map/slice | solution.py:55
  308.2 26.3 %reshape.181 = bf16[6,4,4,4,3,4,1536]{6,5,4,3,2,1,0:T(4,128)(2,1)} reshape(bf16[24,16,12,1536]{3,2,1,0:T(8,128)(2,1)} %get-tuple-element.357) | data formatting | bytes 28311552 | tf_op jit(solution)/shard_map/reshape | solution.py:28
  334.5 12.7 %copy.130 = bf16[6,4,4,4,3,4,1536]{6,5,3,1,4,2,0:T(4,128)(2,1)} copy(bf16[6,4,4,4,3,4,1536]{6,5,4,3,2,1,0:T(4,128)(2,1)} %reshape.181) | data formatting | bytes 28311552 | tf_op jit(solution)/shard_map/reshape | solution.py:28
  347.3 28.4 %reshape_reshape.13 = bf16[6,4,3,64,12,128]{5,4,3,2,1,0:T(8,128)(2,1)} reshape(bf16[6,4,3,4,4,4,1536]{6,5,4,3,2,1,0:T(4,128)(2,1)} %bitcast.134) | data formatting | bytes 28311552 | tf_op jit(solution)/shard_map/reshape;reshape | solution.py:54
  375.6 15.6 %copy.85 = bf16[6,4,3,64,12,128]{5,3,4,1,0,2:T(8,128)(2,1)} copy(bf16[6,4,3,64,12,128]{5,4,3,2,1,0:T(8,128)(2,1)} %reshape_reshape.13) | data formatting | bytes 28311552 | tf_op jit(solution)/shard_map/while | solution.py:102
  391.3 172.4 %while.28 = (s32[]{:T(128)}, f32[8,12,64]{2,1,0:T(8,128)S(1)}, pred[27,8]{1,0:T(8,128)(4,1)S(1)}, s32[27]{0:T(128)S(1)}, bf16[6,4,3,64,12,128]{5,3,4,1,0,2:T(8,1...) while((s32[]{:T(128)}, f32[8,12,64]{2,1,0:T(8,128)S(1)}, ...), condition=%wide.region_3.4_spmd, body=%wide.region_1.3_spmd.sunk | while | flops 101842976 | bytes 6390297 | solution.py:102
  563.7 4.8 fusion.15
  570.2 26.3 %reshape.183 = bf16[6,4,4,4,3,4,1536]{6,5,4,3,2,1,0:T(4,128)(2,1)} reshape(bf16[24,16,12,1536]{3,2,1,0:T(8,128)(2,1)} %get-tuple-element.356) | data formatting | bytes 28311552 | tf_op jit(solution)/shard_map/reshape | solution.py:28
  596.5 12.7 %copy.129 = bf16[6,4,4,4,3,4,1536]{6,5,3,1,4,2,0:T(4,128)(2,1)} copy(bf16[6,4,4,4,3,4,1536]{6,5,4,3,2,1,0:T(4,128)(2,1)} %reshape.183) | data formatting | bytes 28311552 | tf_op jit(solution)/shard_map/reshape | solution.py:28
  609.2 28.4 %reshape_reshape.14 = bf16[6,4,3,64,12,128]{5,4,3,2,1,0:T(8,128)(2,1)} reshape(bf16[6,4,3,4,4,4,1536]{6,5,4,3,2,1,0:T(4,128)(2,1)} %bitcast.135) | data formatting | bytes 28311552 | tf_op jit(solution)/shard_map/reshape;reshape | solution.py:55
  637.6 15.6 %copy.93 = bf16[6,4,3,64,12,128]{5,3,4,1,0,2:T(8,128)(2,1)} copy(bf16[6,4,3,64,12,128]{5,4,3,2,1,0:T(8,128)(2,1)} %reshape_reshape.14) | data formatting | bytes 28311552 | tf_op jit(solution)/shard_map/while | solution.py:123
  653.1 239.0 %while.29 = (s32[]{:T(128)}, f32[8,64,12,128]{3,1,2,0:T(8,128)S(1)}, f32[8,12,64]{2,1,0:T(8,128)S(1)}, s32[27]{0:T(128)S(1)}, bf16[6,4,3,64,12,128]{5,3,4,1,0,2:...) while((s32[]{:T(128)}, ...), condition=%wide.region_7.8_spmd, body=%wide.region_5.7_spmd.sunk | while | flops 205258784 | bytes 26886740 | solution.py:123
  656.6 2.7 constant_dynamic-slice_fusion.6
  895.9 3.3 copy.97
  (411 shorter events, 279.7 us)
Async XLA Ops:
  7.2 218.8 %all-reduce.3.cloned.1.call-start = ((), (), s32[]{:S(2)}) async-start(), calls=%async_computation | async-start | bytes 3145728 | tf_op jit(solution)/shard_map/psum | solution.py:159
  10.2 72.3 %collective-permute-start = (bf16[16,8,4,3072]{3,2,1,0:T(4,128)(2,1)S(1)}, bf16[16,8,4,3072]{3,2,1,0:T(4,128)(2,1)S(1)}, u32[]{:S(2)}, u32[]{:S(2)}) collective-permute-start(bf16[16,8,4,3072]{3,2,1,0:T(4,128)(2,1)S(1)} %constant_dynamic-update-slice_fusion), channel_id=1, source_target_pairs={{0,4},{4,8},{8,12},{1,5},{5,9},{9,13},{2,6},{6,10},{10,14},{3,7},{... | collective-permute-start | bytes 9437192 | tf_op jit(solution)/shard_map/ppermute | solution.py:18
  15.4 71.5 %collective-permute-start.1 = (bf16[16,8,4,3072]{3,2,1,0:T(4,128)(2,1)S(1)}, bf16[16,8,4,3072]{3,2,1,0:T(4,128)(2,1)S(1)}, u32[]{:S(2)}, u32[]{:S(2)}) collective-permute-start(bf16[16,8,4,3072]{3,2,1,0:T(4,128)(2,1)S(1)} %constant_dynamic-update-slice_fusion), channel_id=1, source_target_pairs={{4,0},{8,4},{12,8},{5,1},{9,5},{13,9},{6,2},{10,6},{14,10},{7,3},{... | collective-permute-start | bytes 9437192 | tf_op jit(solution)/shard_map/ppermute | solution.py:19
  82.5 4.3 copy-start.3
  100.7 134.7 %collective-permute-start.2 = (bf16[16,4,12,3072]{3,2,1,0:T(8,128)(2,1)}, bf16[16,4,12,3072]{3,2,1,0:T(8,128)(2,1)}, u32[]{:S(2)}, u32[]{:S(2)}) collective-permute-start(bf16[16,4,12,3072]{3,2,1,0:T(8,128)(2,1)} %get-tuple-element.358), channel_id=1, source_target_pairs={{0,2},{1,3},{4,6},{5,7},{8,10},{9,11},{12,14},{13,15},{16,18},{17,... | collective-permute-start | bytes 14155784 | tf_op jit(solution)/shard_map/ppermute | solution.py:18
  104.5 130.8 %collective-permute-start.3 = (bf16[16,4,12,3072]{3,2,1,0:T(8,128)(2,1)}, bf16[16,4,12,3072]{3,2,1,0:T(8,128)(2,1)}, u32[]{:S(2)}, u32[]{:S(2)}) collective-permute-start(bf16[16,4,12,3072]{3,2,1,0:T(8,128)(2,1)} %get-tuple-element.359), channel_id=1, source_target_pairs={{2,0},{3,1},{6,4},{7,5},{10,8},{11,9},{14,12},{15,13},{18,16},{19,... | collective-permute-start | bytes 14155784 | tf_op jit(solution)/shard_map/ppermute | solution.py:19
  118.8 37.4 %copy-start.10 = (s32[256]{0:T(256)S(1)}, s32[256]{0:T(256)}, u32[]{:S(2)}) copy-start(s32[256]{0:T(256)} %param.17) | copy-start | bytes 3076
  156.2 4.0 copy-start.5
  173.3 7.2 slice-start
  175.5 5.0 slice-start.1
  177.8 2.8 copy-start
  375.6 15.6 %copy-start.7 = (bf16[8,64,12,128]{3,1,2,0:T(8,128)(2,1)S(1)}, bf16[8,64,12,128]{3,1,2,0:T(8,128)(2,1)}, u32[]{:S(2)}) copy-start(bf16[8,64,12,128]{3,1,2,0:T(8,128)(2,1)} %copy.86) | copy-start | bytes 4718596
  391.3 177.3 %copy-start.9 = (bf16[256,1536]{0,1:T(8,128)(2,1)S(1)}, bf16[256,1536]{0,1:T(8,128)(2,1)}, u32[]{:S(2)}) copy-start(bf16[256,1536]{0,1:T(8,128)(2,1)} %copy.88) | copy-start | bytes 2359300
  563.7 4.8 copy-start.1
  656.6 2.7 copy-start.8
  665.4 2.7 copy-start.8
  674.3 2.7 copy-start.8
  683.1 2.7 copy-start.8
  692.0 2.7 copy-start.8
  700.8 2.7 copy-start.8
  709.7 2.7 copy-start.8
  718.5 2.7 copy-start.8
  727.4 2.7 copy-start.8
  736.2 2.7 copy-start.8
  745.1 2.7 copy-start.8
  762.8 2.7 copy-start.8
  771.6 2.7 copy-start.8
  798.2 2.7 copy-start.8
  824.7 2.7 copy-start.8
  851.3 2.7 copy-start.8
  877.8 2.7 copy-start.8
  886.7 2.7 copy-start.8
  (12 other events, 30.2 us)
Sparse Core Ops, SparseCore 0:
  166.0 59.9 all-reduce.2
where the time goes:
time: 919 us; the launch traced here: 906 us
  local copies, waits for them, and re-layouts  388 us (42%)
  loops' own time  166 us (18%)
  matrix products  121 us (13%)
  waiting for transfers between devices  80.8 us (9%)
  other arithmetic  65.6 us (7%)
  blocking collectives  57.9 us (6%)
  between operations  14.5 us (2%)
  starting transfers between devices  11.6 us (1%)
    dynamic_slice x54, local copies, waits for them, and re-layouts, window_block(): lax.dynamic_slice(grid, starts, (time_tiles, row_tiles, col_tiles, volume...  114 us
    another operation x1, loops' own time, shards(): lax.scan(peak_slot, jnp.max(cross_scores, axis=3), (slot_list, inside.T))  87.3 us
    reshape x5, local copies, waits for them, and re-layouts, into_tiles(): field.reshape(time_tiles, TILE, row_tiles, TILE, col_tiles, TILE, field.s...  81.3 us
    another operation x1, loops' own time, shards(): lax.scan(add_slot, (text_part, jnp.sum(cross_probs, axis=3)), (slot_list,...  79.1 us
    ppermute x2, waiting for transfers between devices, with_halo(): before = lax.ppermute(last, axis, up)  65.8 us
    concatenate x2, other arithmetic, with_halo(): array = jnp.concatenate([before, array, after], axis=dim)  53.6 us
    dot_general x54, matrix products, slot_scores(): jnp.einsum('qahd,qbhd->qhab', query_tiles, picked, preferred_element_type...  53 us
    dot_general x27, matrix products, add_slot(): jnp.einsum('qhab,qbhd->qahd', probs.astype(jnp.bfloat16), picked, preferr...  44 us
  transfers between devices with their start and end apart: 5, of which 3 were waited for; matrix products, arithmetic and copies ran while one was open for 7% of the time, Pallas kernels for 0%

commit v1 on v0

--- a/solution.py
+++ b/solution.py
@@ -6,6 +6,11 @@
 
 HD = 128
 TILE = 4
+
+
+def by_each_axis(array_2, one, other):
+    inner = lax.psum(array_2, one)
+    return lax.psum(inner, other)
 
 
 def with_halo(array, sides, width):
@@ -156,7 +161,7 @@
         text_values,
         preferred_element_type=jnp.float32,
     )
-    whole_summed, whole_total = lax.psum((far_summed, far_total), ("tm", "height"))
+    whole_summed, whole_total = by_each_axis((far_summed, far_total), "height", "tm")
     finished = (whole_summed + near_summed) / (whole_total + near_total)[:, :, None]
     out_text = finished.astype(jnp.bfloat16).reshape(text_count, features)
     return (out_video, out_text)

time: 919 us -> 949 us (1.033)
  starting transfers between devices: 11.6 us -> 24.3 us
  loops' own time: 166 us -> 176 us
    psum x1 -> x2, waiting for transfers between devices: 10.6 us -> 33.6 us  [the longest x1 33.6 us: by_each_axis(): return lax.psum(inner, other)]
    another operation x1, loops' own time: 79.1 us -> 96.7 us  [shards(): lax.scan(add_slot, (text_part, jnp.sum(cross_probs, axis=3)), (slot_list,...]
    ppermute x2, waiting for transfers between devices: 65.8 us -> 49.8 us  [with_halo(): before = lax.ppermute(last, axis, up)]
    psum x1 -> x2, starting transfers between devices: 0.04 us -> 11.4 us  [the longest x1 11.3 us: by_each_axis(): return lax.psum(inner, other)]
    psum x1 -> x2, blocking collectives: 26.5 us -> 20.2 us  [the longest x1 16.8 us: by_each_axis(): return lax.psum(inner, other)]
  transfers between devices with their start and end apart: 5 -> 6, of which waited for: 3 -> 3; matrix products, arithmetic and copies ran while one was open for 7% -> 7% of each run, Pallas kernels for 0% -> 0%
where the time goes in v1:
time: 949 us; the launch traced here: 934 us
  local copies, waits for them, and re-layouts  387 us (41%)
  loops' own time  176 us (19%)
  matrix products  122 us (13%)
  waiting for transfers between devices  89.3 us (9%)
  other arithmetic  71.5 us (8%)
  blocking collectives  49.7 us (5%)
  starting transfers between devices  24.3 us (3%)
  between operations  14.7 us (2%)
    dynamic_slice x54, local copies, waits for them, and re-layouts, window_block(): lax.dynamic_slice(grid, starts, (time_tiles, row_tiles, col_tiles, volume...  114 us
    another operation x1, loops' own time, shards(): lax.scan(add_slot, (text_part, jnp.sum(cross_probs, axis=3)), (slot_list,...  96.7 us
    reshape x5, local copies, waits for them, and re-layouts, into_tiles(): field.reshape(time_tiles, TILE, row_tiles, TILE, col_tiles, TILE, field.s...  81.3 us
    another operation x1, loops' own time, shards(): lax.scan(peak_slot, jnp.max(cross_scores, axis=3), (slot_list, inside.T))  79.7 us
    concatenate x2, other arithmetic, with_halo(): array = jnp.concatenate([before, array, after], axis=dim)  54.6 us
    dot_general x54, matrix products, slot_scores(): jnp.einsum('qahd,qbhd->qhab', query_tiles, picked, preferred_element_type...  53 us
    ppermute x2, waiting for transfers between devices, with_halo(): before = lax.ppermute(last, axis, up)  49.8 us
    dot_general x27, matrix products, add_slot(): jnp.einsum('qhab,qbhd->qahd', probs.astype(jnp.bfloat16), picked, preferr...  44 us
  transfers between devices with their start and end apart: 6, of which 3 were waited for; matrix products, arithmetic and copies ran while one was open for 7% of the time, Pallas kernels for 0%

profile of v1, /device:TPU:0, one launch (start us, length us, event | category | flops | bytes accessed | tf_op | source)
XLA Modules:
  0.0 934.2 jit_solution(8284217873482483861)
XLA Ops:
  10.2 6.5 collective-permute-start
  18.1 4.2 reshape.186
  26.8 5.9 multiply_reduce_fusion
  32.7 49.8 %collective-permute-done = bf16[16,8,4,3072]{3,2,1,0:T(4,128)(2,1)} collective-permute-done((bf16[16,8,4,3072]{3,2,1,0:T(4,128)(2,1)S(1)}, bf16[16,8,4,3072]{3,2,1,0:T(4,128)(2,1)}, u32[]{:S(2)}, u32[]{:S(2)}) %collective-permute-start) | collective-permute-done | bytes 3145760 | tf_op jit(solution)/shard_map/ppermute | solution.py:23
  82.5 5.8 collective-permute-done.1
  88.3 8.1 pad_maximum_fusion
  96.4 5.2 fusion.69
  101.7 3.9 collective-permute-start.2
  109.3 4.2 reshape.187
  113.5 29.5 %pmax.7 = f32[12,256]{1,0:T(8,128)S(1)} all-reduce(f32[12,256]{1,0:T(8,128)S(1)} %get-tuple-element.360), channel_id=1, replica_groups=mesh['grp'=2,'tm'=4,'height'=2,'head'=2] {'tm','height'}, use_global_device_ids=true, to_apply=%region_9.10 | all-reduce | flops 3072 | bytes 24576 | tf_op jit(solution)/shard_map/pmax | solution.py:146
  143.0 6.3 fusion.44
  149.3 11.3 %all-reduce.6.cloned.1.call-start = ((), (), s32[]{:S(2)}) async-start(), calls=%async_computation.1 | async-start | bytes 3145728 | tf_op jit(solution)/shard_map/psum | solution.py:13
  163.9 4.3 reshape_reshape.12
  170.3 3.7 fusion.70
  174.0 3.8 bitcast_reduce_fusion.1
  181.7 3.6 fusion.13
  188.7 16.8 %psum.31 = f32[256,12]{0,1:T(8,128)S(1)} all-reduce(f32[256,12]{0,1:T(8,128)S(1)} %psum.30), channel_id=1, replica_groups=mesh['grp'=2,'tm'=4,'height'=2,'head'=2] {'tm'}, use_global_device_ids=true, to_apply=%region_15.16 | all-reduce | flops 3072 | bytes 24576 | tf_op jit(solution)/shard_map/psum | solution.py:13
  208.3 33.6 %all-reduce.6.cloned.1.call-done = f32[256,12,128]{2,0,1:T(8,128)} async-done(((f32[256,12,128]{2,0,1:T(8,128)}), f32[256,12,128]{2,0,1:T(8,128)}) %all-reduce.6.cloned.1.call-update) | async-done | bytes 1572880 | tf_op jit(solution)/shard_map/psum | solution.py:13
  242.0 4.8 fusion.36
  251.4 46.6 %select_maximum_fusion = bf16[24,16,12,3072]{3,2,1,0:T(8,128)(2,1)} fusion(bf16[16,4,12,3072]{3,2,1,0:T(8,128)(2,1)} %collective-permute-done.3, bf16[16,4,12,3072]{3,2,1,0:T(8,128)(2,1)} %collective-permute-done.2, bf16[16,8,4,3072]{3,2,1,0:T(4,128)(2,1)} %collective-permute-done.1, bf16[16,8,4,3072]{3,2,1,0:T(4,128)(2,1)S(1)} %constant_dynamic-update-slice_fusion, ...), kind=kLoop, calls=%fused_computation.19 | loop fusion | flops 254803968 | bytes 47185920 | tf_op jit(solution)/shard_map/concatenate | solution.py:25
  297.9 26.2 %fusion.68 = (bf16[24,16,12,1536]{3,2,1,0:T(8,128)(2,1)}, bf16[24,16,12,1536]{3,2,1,0:T(8,128)(2,1)}) fusion(bf16[24,16,12,3072]{3,2,1,0:T(8,128)(2,1)} %select_maximum_fusion), kind=kLoop, calls=%fused_computation.106 | loop fusion | bytes 56623104 | tf_op jit(solution)/shard_map/slice | solution.py:60
  324.2 26.3 %reshape.181 = bf16[6,4,4,4,3,4,1536]{6,5,4,3,2,1,0:T(4,128)(2,1)} reshape(bf16[24,16,12,1536]{3,2,1,0:T(8,128)(2,1)} %get-tuple-element.357) | data formatting | bytes 28311552 | tf_op jit(solution)/shard_map/reshape | solution.py:33
  350.4 12.7 %copy.130 = bf16[6,4,4,4,3,4,1536]{6,5,3,1,4,2,0:T(4,128)(2,1)} copy(bf16[6,4,4,4,3,4,1536]{6,5,4,3,2,1,0:T(4,128)(2,1)} %reshape.181) | data formatting | bytes 28311552 | tf_op jit(solution)/shard_map/reshape | solution.py:33
  363.2 28.4 %reshape_reshape.13 = bf16[6,4,3,64,12,128]{5,4,3,2,1,0:T(8,128)(2,1)} reshape(bf16[6,4,3,4,4,4,1536]{6,5,4,3,2,1,0:T(4,128)(2,1)} %bitcast.134) | data formatting | bytes 28311552 | tf_op jit(solution)/shard_map/reshape;reshape | solution.py:59
  391.6 15.7 %copy.85 = bf16[6,4,3,64,12,128]{5,3,4,1,0,2:T(8,128)(2,1)} copy(bf16[6,4,3,64,12,128]{5,4,3,2,1,0:T(8,128)(2,1)} %reshape_reshape.13) | data formatting | bytes 28311552 | tf_op jit(solution)/shard_map/while | solution.py:107
  407.2 164.3 %while.28 = (s32[]{:T(128)}, f32[8,12,64]{2,1,0:T(8,128)S(1)}, pred[27,8]{1,0:T(8,128)(4,1)S(1)}, s32[27]{0:T(128)S(1)}, bf16[6,4,3,64,12,128]{5,3,4,1,0,2:T(8,1...) while((s32[]{:T(128)}, f32[8,12,64]{2,1,0:T(8,128)S(1)}, ...), condition=%wide.region_3.4_spmd, body=%wide.region_1.3_spmd.sunk | while | flops 101842976 | bytes 6390297 | solution.py:107
  571.6 4.8 fusion.15
  578.0 26.3 %reshape.183 = bf16[6,4,4,4,3,4,1536]{6,5,4,3,2,1,0:T(4,128)(2,1)} reshape(bf16[24,16,12,1536]{3,2,1,0:T(8,128)(2,1)} %get-tuple-element.356) | data formatting | bytes 28311552 | tf_op jit(solution)/shard_map/reshape | solution.py:33
  604.3 12.7 %copy.129 = bf16[6,4,4,4,3,4,1536]{6,5,3,1,4,2,0:T(4,128)(2,1)} copy(bf16[6,4,4,4,3,4,1536]{6,5,4,3,2,1,0:T(4,128)(2,1)} %reshape.183) | data formatting | bytes 28311552 | tf_op jit(solution)/shard_map/reshape | solution.py:33
  617.0 28.4 %reshape_reshape.14 = bf16[6,4,3,64,12,128]{5,4,3,2,1,0:T(8,128)(2,1)} reshape(bf16[6,4,3,4,4,4,1536]{6,5,4,3,2,1,0:T(4,128)(2,1)} %bitcast.135) | data formatting | bytes 28311552 | tf_op jit(solution)/shard_map/reshape;reshape | solution.py:60
  645.4 15.5 %copy.93 = bf16[6,4,3,64,12,128]{5,3,4,1,0,2:T(8,128)(2,1)} copy(bf16[6,4,3,64,12,128]{5,4,3,2,1,0:T(8,128)(2,1)} %reshape_reshape.14) | data formatting | bytes 28311552 | tf_op jit(solution)/shard_map/while | solution.py:128
  660.9 259.0 %while.29 = (s32[]{:T(128)}, f32[8,64,12,128]{3,1,2,0:T(8,128)S(1)}, f32[8,12,64]{2,1,0:T(8,128)S(1)}, s32[27]{0:T(128)S(1)}, bf16[6,4,3,64,12,128]{5,3,4,1,0,2:...) while((s32[]{:T(128)}, ...), condition=%wide.region_7.8_spmd, body=%wide.region_5.7_spmd.sunk | while | flops 205258784 | bytes 26886740 | solution.py:128
  (408 shorter events, 288.1 us)
Async XLA Ops:
  7.2 166.8 %all-reduce.4.cloned.1.call-start = ((), (), s32[]{:S(2)}) async-start(), calls=%async_computation | async-start | bytes 3145728 | tf_op jit(solution)/shard_map/psum | solution.py:12
  10.2 16.6 %copy-start.9 = (s32[256]{0:T(256)S(1)}, s32[256]{0:T(256)}, u32[]{:S(2)}) copy-start(s32[256]{0:T(256)} %param.17) | copy-start | bytes 3076
  10.2 72.3 %collective-permute-start = (bf16[16,8,4,3072]{3,2,1,0:T(4,128)(2,1)S(1)}, bf16[16,8,4,3072]{3,2,1,0:T(4,128)(2,1)}, u32[]{:S(2)}, u32[]{:S(2)}) collective-permute-start(bf16[16,8,4,3072]{3,2,1,0:T(4,128)(2,1)S(1)} %constant_dynamic-update-slice_fusion), channel_id=1, source_target_pairs={{0,4},{4,8},{8,12},{1,5},{5,9},{9,13},{2,6},{6,10},{10,14},{3,7},{... | collective-permute-start | bytes 9437192 | tf_op jit(solution)/shard_map/ppermute | solution.py:23
  16.8 71.5 %collective-permute-start.1 = (bf16[16,8,4,3072]{3,2,1,0:T(4,128)(2,1)S(1)}, bf16[16,8,4,3072]{3,2,1,0:T(4,128)(2,1)}, u32[]{:S(2)}, u32[]{:S(2)}) collective-permute-start(bf16[16,8,4,3072]{3,2,1,0:T(4,128)(2,1)S(1)} %constant_dynamic-update-slice_fusion), channel_id=1, source_target_pairs={{4,0},{8,4},{12,8},{5,1},{9,5},{13,9},{6,2},{10,6},{14,10},{7,3},{... | collective-permute-start | bytes 9437192 | tf_op jit(solution)/shard_map/ppermute | solution.py:24
  96.4 10.4 %copy-start.2 = (bf16[256,1536]{0,1:T(8,128)(2,1)S(1)}, bf16[256,1536]{0,1:T(8,128)(2,1)}, u32[]{:S(2)}) copy-start(bf16[256,1536]{0,1:T(8,128)(2,1)} %copy.79) | copy-start | bytes 2359300
  96.4 10.4 %copy-start.4 = (bf16[256,1536]{0,1:T(8,128)(2,1)S(1)}, bf16[256,1536]{0,1:T(8,128)(2,1)}, u32[]{:S(2)}) copy-start(bf16[256,1536]{0,1:T(8,128)(2,1)} %copy.98) | copy-start | bytes 2359300
  101.7 149.7 %collective-permute-start.2 = (bf16[16,4,12,3072]{3,2,1,0:T(8,128)(2,1)}, bf16[16,4,12,3072]{3,2,1,0:T(8,128)(2,1)}, u32[]{:S(2)}, u32[]{:S(2)}) collective-permute-start(bf16[16,4,12,3072]{3,2,1,0:T(8,128)(2,1)} %get-tuple-element.358), channel_id=1, source_target_pairs={{0,2},{1,3},{4,6},{5,7},{8,10},{9,11},{12,14},{13,15},{16,18},{17,... | collective-permute-start | bytes 14155784 | tf_op jit(solution)/shard_map/ppermute | solution.py:23
  105.5 145.8 %collective-permute-start.3 = (bf16[16,4,12,3072]{3,2,1,0:T(8,128)(2,1)}, bf16[16,4,12,3072]{3,2,1,0:T(8,128)(2,1)}, u32[]{:S(2)}, u32[]{:S(2)}) collective-permute-start(bf16[16,4,12,3072]{3,2,1,0:T(8,128)(2,1)} %get-tuple-element.359), channel_id=1, source_target_pairs={{2,0},{3,1},{6,4},{7,5},{10,8},{11,9},{14,12},{15,13},{18,16},{19,... | collective-permute-start | bytes 14155784 | tf_op jit(solution)/shard_map/ppermute | solution.py:24
  149.3 92.7 %all-reduce.6.cloned.1.call-start = ((), (), s32[]{:S(2)}) async-start(), calls=%async_computation.1 | async-start | bytes 3145728 | tf_op jit(solution)/shard_map/psum | solution.py:13
  174.0 3.8 copy-start.1
  391.6 15.7 %copy-start.6 = (bf16[8,64,12,128]{3,1,2,0:T(8,128)(2,1)S(1)}, bf16[8,64,12,128]{3,1,2,0:T(8,128)(2,1)}, u32[]{:S(2)}) copy-start(bf16[8,64,12,128]{3,1,2,0:T(8,128)(2,1)} %copy.86) | copy-start | bytes 4718596
  407.2 169.1 %copy-start.8 = (bf16[256,1536]{0,1:T(8,128)(2,1)S(1)}, bf16[256,1536]{0,1:T(8,128)(2,1)}, u32[]{:S(2)}) copy-start(bf16[256,1536]{0,1:T(8,128)(2,1)} %copy.88) | copy-start | bytes 2359300
  571.6 4.8 copy-start
  665.1 2.7 copy-start.7
  674.7 2.7 copy-start.7
  684.3 2.7 copy-start.7
  693.9 2.7 copy-start.7
  703.5 2.7 copy-start.7
  713.0 2.7 copy-start.7
  722.6 2.7 copy-start.7
  732.2 2.7 copy-start.7
  741.8 2.7 copy-start.7
  751.4 2.7 copy-start.7
  761.0 2.7 copy-start.7
  770.6 2.7 copy-start.7
  780.2 2.7 copy-start.7
  789.8 2.7 copy-start.7
  799.4 2.7 copy-start.7
  809.0 2.7 copy-start.7
  818.6 2.7 copy-start.7
  828.1 2.7 copy-start.7
  914.5 2.7 copy-start.7
  (10 other events, 26.1 us)
Sparse Core Ops, SparseCore 0:
  149.4 18.5 all-reduce.3
  174.1 67.7 all-reduce.5
